TPU v7x, 256 devices: a whole 4x4x8 slice. The times are simulated.
256 devices in a mesh: ctx: 32 (over y_hi, z, core), ch: 8 (over y_lo, x).
Axes of the slice: x: 4, y: 4 (y_hi: 2, y_lo: 2; y = y_hi * 2 + y_lo), z: 8, core: 2. Of those that a mesh axis runs over, the one named last changes fastest.
Arguments:
- streams: bfloat16 [16384, 3, 2048], P('ctx', None, 'ch'), may hold values from -6 to 6
- short_taps: float32 [3, 3, 2048], P(None, None, 'ch'), may hold values from -3 to 3
- filters: bfloat16 [16384, 2048], P('ctx', 'ch'), may hold values from -1 to 1, as said below
- skip_gain: float32 [2048], P('ch'), may hold values from 0.2 to 0.6
- out_weight: bfloat16 [2048, 4096], P('ch'), may hold values from -0.1875 to 0.1875
Outputs:
- output: bfloat16 [16384, 4096], P('ctx', 'ch')
Inputs may be any that keep to these rules, and one draw needn't show every extreme that they name: `filters`: filter taps of every channel and lag.
All inputs are finite; a program needn't handle non-finite values.
Results may differ from a plain program's by a relative error of at most 0.017.
Values may be sent and summed in bfloat16 or wider, within the bound.
A program may use at most 128 MiB of HBM per device.

v0:
```python
import math

import jax
import jax.numpy as jnp
from jax import lax
from jax.sharding import PartitionSpec as P


def passed_along(value, axis, steps):
    count = lax.axis_size(axis)
    initial, last = (max(0, -steps), min(count, count - steps))
    return lax.ppermute(value, axis, [(source, source + steps) for source in range(initial, last)])


def forward_table(size):
    half = size // 2
    rows = jnp.arange(size, dtype=jnp.int32)[:, None]
    cols = jnp.arange(size, dtype=jnp.int32)[None, :]
    freq = jnp.where(cols < half, cols, cols - half)
    phase = rows * freq % size
    angle = phase.astype(jnp.float32) * (2.0 * math.pi / size)
    cosine = jnp.cos(angle)
    sine = -jnp.sin(angle)
    nyquist = jnp.where(rows % 2 == 0, 1.0, -1.0).astype(jnp.float32)
    table = jnp.where(cols < half, cosine, jnp.where(cols == half, nyquist, sine))
    return table.astype(jnp.bfloat16)


def inverse_table(size):
    half = size // 2
    rows = jnp.arange(size, dtype=jnp.int32)[:, None]
    places = half + jnp.arange(half, dtype=jnp.int32)[None, :]
    freq = jnp.where(rows < half, rows, rows - half)
    phase = places * freq % size
    angle = phase.astype(jnp.float32) * (2.0 * math.pi / size)
    weight = jnp.where(freq == 0, 1.0, 2.0).astype(jnp.float32) / size
    cosine = weight * jnp.cos(angle)
    sine = -weight * jnp.sin(angle)
    nyquist = jnp.where(places % 2 == 0, 1.0, -1.0).astype(jnp.float32) / size
    table = jnp.where(rows < half, cosine, jnp.where(rows == half, nyquist, sine))
    return table.astype(jnp.bfloat16)


def spectrum_product(left, right):
    half = left.shape[-1] // 2
    right = right.astype(jnp.float32)
    left_re, left_im = (left[..., :half], left[..., half:])
    right_re, right_im = (right[..., :half], right[..., half:])
    inside = jnp.arange(half, dtype=jnp.int32) > 0
    real_part = left_re * right_re - jnp.where(inside, left_im * right_im, 0.0)
    imag_part = jnp.where(inside, left_re * right_im + left_im * right_re, left_im * right_im)
    return jnp.concatenate([real_part, imag_part], axis=-1)


def block_spectrum(block, head_table):
    return lax.dot_general(
        block, head_table, (((0,), (0,)), ((), ())), preferred_element_type=jnp.float32
    )


def keep_carry(carry):
    return carry


def local(streams, short_taps, filters, skip_gain, out_weight):
    block_rows = streams.shape[0]
    channels = streams.shape[2]
    width = 2 * block_rows
    position = lax.axis_index("ctx")
    edge_rows = passed_along(streams[block_rows - 2 :], "ctx", 1)
    extended = jnp.concatenate([edge_rows, streams], axis=0)
    mixed = short_taps[0][None] * extended[2:].astype(jnp.float32)
    mixed = mixed + short_taps[1][None] * extended[1 : block_rows + 1].astype(jnp.float32)
    mixed = mixed + short_taps[2][None] * extended[:block_rows].astype(jnp.float32)
    inner = (mixed[:, 0, :] * mixed[:, 1, :]).astype(jnp.bfloat16)
    forward = forward_table(width)
    backward = inverse_table(width)
    head_table = forward[:block_rows]
    before = passed_along(filters, "ctx", 1)
    window = jnp.concatenate([before, filters], axis=0)
    own_spectrum = block_spectrum(window, forward).astype(jnp.bfloat16)
    spectra = lax.all_gather(own_spectrum[None], "ctx", axis=0, tiled=True)
    empty = jnp.zeros((channels, width), jnp.float32)
    piece = lax.all_gather(inner, "ctx", axis=0, tiled=True)
    count = piece.shape[0] // block_rows

    def one_tile(offset, running):
        segment = lax.dynamic_slice_in_dim(piece, offset * block_rows, block_rows, 0)

        def add_tile(current):
            spectrum = block_spectrum(segment, head_table)
            return current + spectrum_product(spectrum, spectra[position - offset])

        return lax.cond(offset <= position, add_tile, keep_carry, running)

    accumulated = lax.fori_loop(0, count, one_tile, empty)
    spectrum_low = accumulated.astype(jnp.bfloat16)
    long_conv = lax.dot_general(
        backward, spectrum_low, (((0,), (1,)), ((), ())), preferred_element_type=jnp.float32
    ).astype(jnp.bfloat16)
    gated = (
        mixed[:, 2, :]
        * (long_conv.astype(jnp.float32) + skip_gain[None, :] * inner.astype(jnp.float32))
    ).astype(jnp.bfloat16)
    partial_term = jnp.dot(gated, out_weight, preferred_element_type=jnp.float32)
    return lax.psum_scatter(
        partial_term.astype(jnp.bfloat16), "ch", scatter_dimension=1, tiled=True
    )


def solution(mesh):
    return jax.shard_map(
        local,
        mesh=mesh,
        in_specs=(
            P("ctx", None, "ch"),
            P(None, None, "ch"),
            P("ctx", "ch"),
            P("ch"),
            P("ch", None),
        ),
        out_specs=P("ctx", "ch"),
        check_vma=False,
    )
```

profile of v0, /device:TPU:1, one launch (start us, length us, event | category | flops | bytes accessed | tf_op | source)
XLA Modules:
  0.0 510.4 jit_solution(12049396825474011906)
XLA Ops:
  6.5 0.9 slice.52
  7.4 4.9 collective-permute-start
  12.3 0.7 slice_bitcast_fusion.3
  13.1 2.6 multiply_add_fusion
  15.7 1.2 copy-done.1
  16.9 0.8 fusion.26
  17.7 0.0 all-gather.5.cloned.1.call-update
  17.7 0.0 all-gather.7.cloned.1.call-start
  17.8 4.2 collective-permute-start.1
  22.0 3.3 collective-permute-done.1
  25.2 18.3 %convolution_convert_fusion.1 = bf16[256,1024]{1,0:T(8,128)(2,1)} fusion(bf16[512,256]{1,0:T(8,128)(2,1)S(1)} %copy-done.3, bf16[512,256]{1,0:T(8,128)(2,1)S(1)} %collective-permute-done.1, bf16[1024]{0:T(1024)(128)(2,1)S(1)} %fusion.40, s32[1024]{0:T(1024)S(1)} %add_select_fusion.4, pred[1024]{0:T(1024)(128)(4,1)S(1)} %get-tuple-element.205, ...), kind=kOutput, calls=%fused_computation.30 | convolution fusion | flops 556007424 | bytes 1056768 | tf_op jit(solution)/shard_map/dot_general | solution.py:56
  43.6 0.0 reduce-scatter.2.cloned.1.call-start
  43.7 17.4 %select_convert_fusion = bf16[1024,1024]{1,0:T(8,128)(2,1)S(1)} fusion(bf16[1024]{0:T(1024)(128)(2,1)S(1)} %fusion.40, s32[1024]{0:T(1024)S(1)} %add_select_fusion.4, pred[1024]{0:T(1024)(128)(4,1)S(1)} %get-tuple-element.205, pred[1024]{0:T(1024)(128)(4,1)S(1)} %get-tuple-element.206), kind=kLoop, calls=%fused_computation.16 | loop fusion | flops 17825792 | bytes 2105344 | tf_op jit(solution)/shard_map/convert_element_type | solution.py:26
  61.1 1.0 slice.69
  62.1 61.9 %all-gather.5.cloned.1.call-done = bf16[16384,1,256]{2,0,1:T(8,128)(2,1)} async-done(((bf16[512,1,256]{2,0,1:T(8,128)(2,1)}), bf16[16384,1,256]{2,0,1:T(8,128)(2,1)}) %all-gather.5.cloned.1.call-update) | async-done | bytes 8388624 | tf_op jit(solution)/shard_map/all_gather | solution.py:84
  124.0 136.6 %all-gather.7.cloned.1.call-done = bf16[8192,1024]{1,0:T(8,128)(2,1)} async-done(((bf16[256,1024]{1,0:T(8,128)(2,1)}), bf16[8192,1024]{1,0:T(8,128)(2,1)}) %all-gather.7.cloned.1.call-update) | async-done | bytes 16777232 | tf_op jit(solution)/shard_map/all_gather | solution.py:82
  260.6 1.1 broadcast_in_dim.108
  261.7 12.3 %while.16 = (s32[]{:T(128)}, f32[256,1024]{1,0:T(8,128)}, s32[]{:T(128)}, bf16[16384,256]{1,0:T(8,128)(2,1)}, bf16[512,1024]{1,0:T(8,128)(2,1)}, /*index=5*/bf16[32,256,1024]{2,1,0:T(8,128)(2,1)}, s32[]{:T(128)}) while((s32[]{:T(128)}, f32[256,1024]{1,0:T(8,128)}, s32[]{:T(128)}, bf16[16384,256]{1,0:T(8,128)(2,1)}, ...), condition=%wide.region_3.4_spmd, body=%wide.region_0.3_spmd.sunk | while | flops 270270976 | bytes 10224887 | solution.py:96
  261.7 5.6 %conditional.2 = (f32[256,1024]{1,0:T(8,128)}) conditional(s32[]{:T(128)} %convert_element_type.154, f32[256,1024]{1,0:T(8,128)} %get-tuple-element.254, (s32[]{:T(128)}, bf16[16384,256]{1,0:T(8,128)(2,1)}, bf16[512,1024]{1,0:T(8,128)(2,1)}, s32[]{:T(128)}, bf16[32,256,1024]{2,1,0:T(8,128)(2,1)}, /*index=5*/f32[256,1024]{1,0:T(8,128)}) %tuple.53), branch_computations={%region_1.1_spmd, %region_2.2_spmd} | conditional | flops 270270976 | bytes 10224748 | solution.py:94
  261.7 1.8 fusion
  263.6 1.2 bitcast_convert_fusion
  264.7 0.2 select_subtract_fusion
  265.0 2.4 maximum_add_fusion
  267.3 5.6 %conditional.2 = (f32[256,1024]{1,0:T(8,128)}) conditional(s32[]{:T(128)} %convert_element_type.154, f32[256,1024]{1,0:T(8,128)} %get-tuple-element.254, (s32[]{:T(128)}, bf16[16384,256]{1,0:T(8,128)(2,1)}, bf16[512,1024]{1,0:T(8,128)(2,1)}, s32[]{:T(128)}, bf16[32,256,1024]{2,1,0:T(8,128)(2,1)}, /*index=5*/f32[256,1024]{1,0:T(8,128)}) %tuple.53), branch_computations={%region_1.1_spmd, %region_2.2_spmd} | conditional | flops 270270976 | bytes 10224748 | solution.py:94
  267.3 1.8 fusion
  269.1 1.2 bitcast_convert_fusion
  270.3 0.2 select_subtract_fusion
  270.5 2.4 maximum_add_fusion
  274.0 10.4 %fusion.28.clone.4 = bf16[512,256]{1,0:T(8,128)(2,1)S(1)} fusion(f32[512,3,256]{2,0,1:T(8,128)} %copy-done.1, f32[1024]{0:T(1024)S(1)} %get-tuple-element.208, bf16[512]{0:T(512)(128)(2,1)S(1)} %select_multiply_fusion.1, s32[1024]{0:T(1024)S(1)} %add_select_fusion.4, s32[512]{0:T(512)S(1)} %iota_add_fusion, ...), kind=kOutput, calls=%fused_computation.53.clone.clone.clone.1 | convolution fusion | flops 279052288 | bytes 2115584 | tf_op jit(solution)/shard_map/dot_general | solution.py:98
  284.5 3.2 convolution_convert_fusion
  287.7 0.0 reduce-scatter.2.cloned.1.call-update
  287.7 216.1 %reduce-scatter.2.cloned.1.call-done = bf16[512,512]{1,0:T(8,128)(2,1)} async-done(((bf16[512,4096]{1,0:T(8,128)(2,1)}), bf16[512,512]{1,0:T(8,128)(2,1)}) %reduce-scatter.2.cloned.1.call-update) | async-done | bytes 524304 | tf_op jit(solution)/shard_map/reduce_scatter | solution.py:106
  (50 shorter events, 0.3 us)
Async XLA Ops:
  6.5 278.0 %copy-start = (bf16[256,4096]{1,0:T(8,128)(2,1)S(1)}, bf16[256,4096]{1,0:T(8,128)(2,1)}, u32[]{:S(2)}) copy-start(bf16[256,4096]{1,0:T(8,128)(2,1)} %param.13) | copy-start | bytes 6291460
  6.5 11.2 %copy-start.3 = (bf16[512,256]{1,0:T(8,128)(2,1)S(1)}, bf16[512,256]{1,0:T(8,128)(2,1)}, u32[]{:S(2)}) copy-start(bf16[512,256]{1,0:T(8,128)(2,1)} %param.11) | copy-start | bytes 786436
  6.5 117.5 %all-gather.5.cloned.1.call-start = ((), (), s32[]{:S(2)}) async-start(), calls=%async_computation.2 | async-start | bytes 8650752 | tf_op jit(solution)/shard_map/all_gather | solution.py:84
  7.4 5.7 %collective-permute-start = (bf16[2,3,256]{2,0,1:T(2,128)(2,1)S(1)}, bf16[2,3,256]{2,0,1:T(2,128)(2,1)S(1)}, u32[]{:S(2)}, u32[]{:S(2)}) collective-permute-start(bf16[2,3,256]{2,0,1:T(2,128)(2,1)S(1)} %slice.52), channel_id=1, source_target_pairs={{0,8},{8,16},{16,24},{24,32},{32,40},{40,48},{48,56},{56,64},{64,7... | collective-permute-start | bytes 9224 | tf_op jit(solution)/shard_map/ppermute | solution.py:12
  15.7 1.2 copy-start.1
  17.7 242.9 %all-gather.7.cloned.1.call-start = ((), (), s32[]{:S(2)}) async-start(), calls=%async_computation.3 | async-start | bytes 17301504 | tf_op jit(solution)/shard_map/all_gather | solution.py:82
  17.8 7.5 %collective-permute-start.1 = (bf16[512,256]{1,0:T(8,128)(2,1)S(1)}, bf16[512,256]{1,0:T(8,128)(2,1)S(1)}, u32[]{:S(2)}, u32[]{:S(2)}) collective-permute-start(bf16[512,256]{1,0:T(8,128)(2,1)S(1)} %copy-done.3), channel_id=1, source_target_pairs={{0,8},{8,16},{16,24},{24,32},{32,40},{40,48},{48,56},{56,64},{64,7... | collective-permute-start | bytes 786440 | tf_op jit(solution)/shard_map/ppermute | solution.py:12
  43.6 460.2 %reduce-scatter.2.cloned.1.call-start = ((), (), s32[]{:S(2)}) async-start(), calls=%async_computation.1 | async-start | bytes 4718592 | tf_op jit(solution)/shard_map/reduce_scatter | solution.py:106
  261.7 12.3 %copy-start.2 = (bf16[512,1,256]{2,0,1:T(8,128)(2,1)S(1)}, bf16[512,1,256]{2,0,1:T(8,128)(2,1)}, u32[]{:S(2)}) copy-start(bf16[512,1,256]{2,0,1:T(8,128)(2,1)} %fusion.26) | copy-start | bytes 786436
  261.7 12.3 %copy-start.4 = (f32[256]{0:T(256)S(1)}, f32[256]{0:T(256)}, u32[]{:S(2)}) copy-start(f32[256]{0:T(256)} %param.12) | copy-start | bytes 3076
Sparse Core Ops, SparseCore 0:
  17.8 106.1 all-gather.4
  126.8 133.8 all-gather.6
  287.9 215.9 reduce-scatter.1
where the time goes:
time: 514 us; the launch traced here: 510 us
  waiting for transfers between devices  418 us (81%)
  matrix products  35.6 us (7%)
  other arithmetic  28.3 us (6%)
  between operations  13.2 us (3%)
  starting transfers between devices  9.17 us (2%)
    reduce_scatter x1, waiting for transfers between devices, local(): lax.psum_scatter(partial_term.astype(jnp.bfloat16), 'ch', scatter_dimensi...  216 us
    all_gather x1, waiting for transfers between devices, local(): spectra = lax.all_gather(own_spectrum[None], 'ctx', axis=0, tiled=True)  137 us
    all_gather x1, waiting for transfers between devices, local(): piece = lax.all_gather(inner, 'ctx', axis=0, tiled=True)  61.9 us
    dot_general x3, matrix products, block_spectrum(): lax.dot_general(block, head_table, (((0,), (0,)), ((), ())), preferred_el...  21.9 us
    convert_element_type x1, other arithmetic, forward_table(): return table.astype(jnp.bfloat16)  17.4 us
    dot_general x1, matrix products, local(): lax.dot_general(backward, spectrum_low, (((0,), (1,)), ((), ())), preferr...  10.4 us
  transfers between devices with their start and end apart: 5, of which 4 were waited for; matrix products, arithmetic and copies ran while one was open for 7% of the time, Pallas kernels for 0%

commit v1 on v0

v1 whole, which is shorter than its diff:
```python
import functools

import jax
import jax.numpy as jnp
import ml_dtypes
import numpy as np
from jax import lax
from jax.experimental import pallas as pl
from jax.experimental.pallas import tpu as pltpu
from jax.sharding import PartitionSpec as P

LANES = 128
GROUP = 4


def half_table(size):
    half = size // 2
    rows = np.arange(half, dtype=np.int64)[:, None]
    cols = np.arange(size, dtype=np.int64)[None, :]
    freq = np.where(cols < half, cols, cols - half)
    angle = (rows * freq % size).astype(np.float64) * (2.0 * np.pi / size)
    nyquist = np.where(rows % 2 == 0, 1.0, -1.0)
    table = np.where(cols < half, np.cos(angle), np.where(cols == half, nyquist, -np.sin(angle)))
    return table.astype(ml_dtypes.bfloat16)


def rows_of(ref):
    blocks, chans, width = ref.shape
    return ref[...].astype(jnp.float32).reshape(blocks * chans, width).astype(jnp.bfloat16)


def conv_kernel(x_ref, h_ref, f_ref, y_ref, xs, hs, low):
    blocks, chans, seg = x_ref.shape
    half = seg
    size = 2 * seg
    tiles = half // LANES
    lead = GROUP - 1
    table = f_ref[...]
    spec = jnp.dot(rows_of(x_ref), table, preferred_element_type=jnp.float32)
    for part in range(2):
        for q in range(tiles):
            at = part * half + q * LANES
            xs[part, q] = spec[:, at : at + LANES].reshape(blocks, chans, LANES)
    filt = jnp.dot(rows_of(h_ref), table, preferred_element_type=jnp.float32)
    lane = lax.broadcasted_iota(jnp.int32, (1, 1, LANES), 2)
    for q in range(tiles):
        inside = (lane > 0) if q == 0 else (lane >= 0)
        weight = jnp.where(inside, 2.0 / size, 1.0 / size).astype(jnp.float32)
        signed = jnp.where(lane % 2 == 0, weight, -weight)
        parts = []
        for part in range(2):
            at = part * half + q * LANES
            block = filt[:, at : at + LANES].reshape(blocks, chans, LANES)
            before = jnp.concatenate(
                [jnp.zeros((1, chans, LANES), jnp.float32), block[: blocks - 1]], axis=0
            )
            parts.append(before * signed + block * weight)
        real, imag = parts
        keep = jnp.broadcast_to(inside, real.shape)
        hs[0, q, lead:] = real
        hs[1, q, lead:] = jnp.where(keep, imag, 0.0)
        hs[2, q, lead:] = jnp.where(keep, real, imag)
        for kind in range(3):
            hs[kind, q, :lead] = jnp.zeros((lead, chans, LANES), jnp.float32)

    def one_tile(q, _):
        def one_group(big, _):
            def one_source(small, total):
                gap = big - small
                xr = [xs[0, q, GROUP * small + b] for b in range(GROUP)]
                xi = [xs[1, q, GROUP * small + b] for b in range(GROUP)]
                gr, gi, g2 = (
                    [hs[kind, q, GROUP * gap + m] for m in range(2 * GROUP - 1)]
                    for kind in range(3)
                )
                total = list(total)
                for a in range(GROUP):
                    for b in range(GROUP):
                        m = a - b + lead
                        total[a] += xr[b] * gr[m] - xi[b] * gi[m]
                        total[GROUP + a] += xr[b] * gi[m] + xi[b] * g2[m]
                return tuple(total)

            zero = jnp.zeros((chans, LANES), jnp.float32)
            total = lax.fori_loop(0, big + 1, one_source, (zero,) * (2 * GROUP))
            rows = pl.ds(pl.multiple_of(big * GROUP * chans, GROUP * chans), GROUP * chans)
            for part in range(2):
                cols = pl.ds(pl.multiple_of(part * half + q * LANES, LANES), LANES)
                piece = jnp.concatenate(total[part * GROUP : (part + 1) * GROUP], axis=0)
                low[rows, cols] = piece.astype(jnp.bfloat16)
            return 0

        return lax.fori_loop(0, blocks // GROUP, one_group, 0)

    lax.fori_loop(0, tiles, one_tile, 0)
    out = lax.dot_general(
        low[...], table, (((1,), (1,)), ((), ())), preferred_element_type=jnp.float32
    )
    y_ref[...] = out.reshape(blocks, chans, seg).astype(jnp.bfloat16)


def long_convolution(x, h, table):
    blocks, chans, seg = x.shape
    tiles = seg // LANES
    return pl.pallas_call(
        conv_kernel,
        out_shape=jax.ShapeDtypeStruct(x.shape, jnp.bfloat16),
        in_specs=[pl.BlockSpec(memory_space=pltpu.VMEM)] * 3,
        out_specs=pl.BlockSpec(memory_space=pltpu.VMEM),
        scratch_shapes=[
            pltpu.VMEM((2, tiles, blocks, chans, LANES), jnp.float32),
            pltpu.VMEM((3, tiles, blocks + GROUP - 1, chans, LANES), jnp.float32),
            pltpu.VMEM((blocks * chans, 2 * seg), jnp.bfloat16),
        ],
        compiler_params=pltpu.CompilerParams(vmem_limit_bytes=32 << 20),
        name="long_convolution",
    )(x, h, table)


def passed_along(value, axis, steps):
    count = lax.axis_size(axis)
    initial, last = (max(0, -steps), min(count, count - steps))
    return lax.ppermute(value, axis, [(source, source + steps) for source in range(initial, last)])


def local(streams, short_taps, filters, skip_gain, out_weight, *, table):
    block_rows = streams.shape[0]
    channels = streams.shape[2]
    count = lax.axis_size("ctx")
    share = channels // count
    edge_rows = passed_along(streams[block_rows - 2 :], "ctx", 1)
    extended = jnp.concatenate([edge_rows, streams], axis=0)
    mixed = short_taps[0][None] * extended[2:].astype(jnp.float32)
    mixed = mixed + short_taps[1][None] * extended[1 : block_rows + 1].astype(jnp.float32)
    mixed = mixed + short_taps[2][None] * extended[:block_rows].astype(jnp.float32)
    inner = (mixed[:, 0, :] * mixed[:, 1, :]).astype(jnp.bfloat16)
    both = jnp.stack([inner.T, filters.T]).reshape(2, count, share, block_rows)
    both = lax.all_to_all(both, "ctx", 1, 1, tiled=True)
    mine = long_convolution(both[0], both[1], table)
    back = lax.all_to_all(mine, "ctx", 0, 0, tiled=True)
    long_conv = back.reshape(channels, block_rows).T
    gated = (
        mixed[:, 2, :]
        * (long_conv.astype(jnp.float32) + skip_gain[None, :] * inner.astype(jnp.float32))
    ).astype(jnp.bfloat16)
    weight = lax.all_to_all(out_weight, "ch", 1, 0, tiled=True)
    every = lax.all_gather(gated, "ch", axis=1, tiled=True)
    return jnp.dot(every, weight, preferred_element_type=jnp.float32).astype(jnp.bfloat16)


def solution(mesh):
    seg = 16384 // mesh.shape["ctx"]
    table = half_table(2 * seg)
    return jax.shard_map(
        functools.partial(local, table=table),
        mesh=mesh,
        in_specs=(
            P("ctx", None, "ch"),
            P(None, None, "ch"),
            P("ctx", "ch"),
            P("ch"),
            P("ch", None),
        ),
        out_specs=P("ctx", "ch"),
        check_vma=False,
    )
```

time: 514 us -> 141 us (0.27)
  the two profiles are of different devices: /device:TPU:1 before, /device:TPU:18 now
where the time goes in v1:
time: 141 us
  blocking collectives  82.7 us (59%)
  waiting for transfers between devices  20.7 us (15%)
  between operations  13.5 us (10%)
  local copies, waits for them, and re-layouts  9.34 us (7%)
  Pallas kernels  4.94 us (4%)
  matrix products  4.27 us (3%)
  other arithmetic  3.44 us (2%)
  starting transfers between devices  1.91 us (1%)
    all_to_all x1, blocking collectives, local(): weight = lax.all_to_all(out_weight, 'ch', 1, 0, tiled=True)  39 us
    all_to_all x1, blocking collectives, local(): both = lax.all_to_all(both, 'ctx', 1, 1, tiled=True)  26.3 us
    all_to_all x1, blocking collectives, local(): back = lax.all_to_all(mine, 'ctx', 0, 0, tiled=True)  17.4 us
    all_gather x1, waiting for transfers between devices, local(): every = lax.all_gather(gated, 'ch', axis=1, tiled=True)  15.9 us
    pallas_call x1, Pallas kernels, long_convolution(): pl.pallas_call(conv_kernel, out_shape=jax.ShapeDtypeStruct(x.shape, jnp.b...  4.94 us
    ppermute x1, waiting for transfers between devices, passed_along(): lax.ppermute(value, axis, [(source, source + steps) for source in range(i...  4.78 us
    dot_general x1, matrix products, local(): jnp.dot(every, weight, preferred_element_type=jnp.float32)  4.27 us
    unnamed x5, local copies, waits for them, and re-layouts  4.09 us
  transfers between devices with their start and end apart: 2, of which 2 were waited for; matrix products, arithmetic and copies ran while one was open for 6% of the time, Pallas kernels for 0%

profile of v1, /device:TPU:18, one launch (start us, length us, event | category | flops | bytes accessed | tf_op | source)
XLA Modules:
  0.0 140.8 jit_solution(6471667916997392452)
XLA Ops:
  6.5 0.0 all-gather.2.cloned.1.call-start
  6.5 0.7 slice.35
  7.2 1.9 %collective-permute-start = (bf16[2,3,256]{2,0,1:T(2,128)(2,1)S(1)}, bf16[2,3,256]{2,0,1:T(2,128)(2,1)S(1)}, u32[]{:S(2)}, u32[]{:S(2)}) collective-permute-start(bf16[2,3,256]{2,0,1:T(2,128)(2,1)S(1)} %slice.35), channel_id=1, source_target_pairs={{0,8},{8,16},{16,24},{24,32},{32,40},{40,48},{48,56},{56,64},{64,7... | collective-permute-start | bytes 9224 | tf_op jit(solution)/shard_map/ppermute | solution.py:123
  9.2 0.7 slice_bitcast_fusion.5
  9.9 1.1 copy.19
  11.0 4.8 %collective-permute-done = bf16[2,3,256]{2,0,1:T(2,128)(2,1)S(1)} collective-permute-done((bf16[2,3,256]{2,0,1:T(2,128)(2,1)S(1)}, bf16[2,3,256]{2,0,1:T(2,128)(2,1)S(1)}, u32[]{:S(2)}, u32[]{:S(2)}) %collective-permute-start) | collective-permute-done | bytes 3104 | tf_op jit(solution)/shard_map/ppermute | solution.py:123
  15.8 2.4 %multiply_add_fusion = f32[512,3,256]{2,0,1:T(8,128)S(1)} fusion(bf16[512,3,256]{2,0,1:T(8,128)(2,1)} %param.6, bf16[2,3,256]{2,0,1:T(2,128)(2,1)S(1)} %collective-permute-done, f32[3,256]{1,0:T(4,128)S(1)} %get-tuple-element.8, f32[3,256]{1,0:T(4,128)S(1)} %get-tuple-element.9, f32[3,256]{1,0:T(4,128)S(1)} %get-tuple-element.7), kind=kLoop, calls=%fused_computation | loop fusion | flops 5505024 | bytes 2371584 | tf_op jit(solution)/shard_map/add | solution.py:135
  18.2 0.1 fusion.6
  18.3 0.1 copy.18
  18.4 0.0 copy-start
  18.5 26.3 %all_to_all.29 = bf16[2,32,8,512]{3,2,0,1:T(8,128)(2,1)S(1)} all-to-all(bf16[2,32,8,512]{3,2,0,1:T(8,128)(2,1)S(1)} %pad_maximum_fusion.1), channel_id=1, replica_groups=mesh['ctx'=32,'ch'=8] {'ctx'}, dimensions={1} | all-to-all | bytes 1048576 | tf_op jit(solution)/shard_map/all_to_all | solution.py:138
  44.8 0.0 copy-done
  44.9 4.9 %long_convolution.1 = bf16[32,8,512]{2,1,0:T(8,128)(2,1)S(1)} custom-call(bf16[32,8,512]{2,1,0:T(8,128)(2,1)S(1)} %get-tuple-element.6.x_ref, bf16[32,8,512]{2,1,0:T(8,128)(2,1)S(1)} %get-tuple-element.5.h_ref, bf16[512,1024]{1,0:T(8,128)(2,1)S(1)} %copy-done), custom_call_target="tpu_custom_call" | custom-call | tf_op jit(solution)/shard_map/long_convolution/pallas_call | solution.py:105
  49.8 0.0 copy-start.1
  49.8 17.4 %all_to_all.30 = bf16[32,8,512]{2,1,0:T(8,128)(2,1)S(1)} all-to-all(bf16[32,8,512]{2,1,0:T(8,128)(2,1)S(1)} %long_convolution.1), channel_id=1, replica_groups=mesh['ctx'=32,'ch'=8] {'ctx'}, dimensions={0} | all-to-all | bytes 524288 | tf_op jit(solution)/shard_map/all_to_all | solution.py:140
  67.3 0.2 copy.22
  67.5 0.0 copy-done.1
  67.5 0.8 fusion.3
  68.3 0.0 all-gather.2.cloned.1.call-update
  68.4 4.1 %copy.23 = bf16[256,4096]{0,1:T(8,128)(2,1)} copy(bf16[256,4096]{1,0:T(8,128)(2,1)} %param.10) | data formatting | bytes 4194304 | tf_op args[4]
  72.4 39.0 %all_to_all.31 = bf16[256,8,512]{0,2,1:T(8,128)(2,1)S(1)} all-to-all(bf16[256,8,512]{0,2,1:T(8,128)(2,1)} %bitcast.41), channel_id=1, replica_groups=mesh['ctx'=32,'ch'=8] {'ch'}, dimensions={1} | all-to-all | bytes 4194304 | tf_op jit(solution)/shard_map/all_to_all | solution.py:146
  111.4 2.4 %copy.24 = bf16[8,256,512]{2,1,0:T(8,128)(2,1)} copy(bf16[8,256,512]{1,2,0:T(8,128)(2,1)S(1)} %bitcast.40) | data formatting | bytes 4194304 | tf_op jit(solution)/shard_map/all_to_all | solution.py:146
  113.8 15.9 %all-gather.2.cloned.1.call-done = bf16[512,2048]{1,0:T(8,128)(2,1)} async-done(((bf16[512,256]{1,0:T(8,128)(2,1)}), bf16[512,2048]{1,0:T(8,128)(2,1)}) %all-gather.2.cloned.1.call-update) | async-done | bytes 2097168 | tf_op jit(solution)/shard_map/all_gather | solution.py:147
  129.7 4.3 %convolution_convert_fusion = bf16[512,512]{1,0:T(8,128)(2,1)} fusion(bf16[512,2048]{1,0:T(8,128)(2,1)} %all-gather.2.cloned.1.call-done, bf16[2048,512]{1,0:T(8,128)(2,1)} %bitcast.42), kind=kOutput, calls=%fused_computation.1 | convolution fusion | flops 1074003968 | bytes 4718592 | tf_op jit(solution)/shard_map/dot_general | solution.py:148
  (3 shorter events, 0.1 us)
Async XLA Ops:
  6.5 123.1 %all-gather.2.cloned.1.call-start = ((), (), s32[]{:S(2)}) async-start(), calls=%async_computation.3 | async-start | bytes 2359296 | tf_op jit(solution)/shard_map/all_gather | solution.py:147
  7.2 8.5 %collective-permute-start = (bf16[2,3,256]{2,0,1:T(2,128)(2,1)S(1)}, bf16[2,3,256]{2,0,1:T(2,128)(2,1)S(1)}, u32[]{:S(2)}, u32[]{:S(2)}) collective-permute-start(bf16[2,3,256]{2,0,1:T(2,128)(2,1)S(1)} %slice.35), channel_id=1, source_target_pairs={{0,8},{8,16},{16,24},{24,32},{32,40},{40,48},{48,56},{56,64},{64,7... | collective-permute-start | bytes 9224 | tf_op jit(solution)/shard_map/ppermute | solution.py:123
  18.4 26.4 %copy-start = (bf16[512,1024]{1,0:T(8,128)(2,1)S(1)}, bf16[512,1024]{1,0:T(8,128)(2,1)}, u32[]{:S(2)}) copy-start(bf16[512,1024]{1,0:T(8,128)(2,1)} %constant.2.clone.f_ref) | copy-start | bytes 3145732
  49.8 17.7 %copy-start.1 = (f32[256]{0:T(256)S(1)}, f32[256]{0:T(256)}, u32[]{:S(2)}) copy-start(f32[256]{0:T(256)} %param.9) | copy-start | bytes 3076
Sparse Core Ops, SparseCore 0:
  68.5 61.1 all-gather.1

commit v2 on v1

v2 whole, which is shorter than its diff:
```python
import functools

import jax
import jax.numpy as jnp
import ml_dtypes
import numpy as np
from jax import lax
from jax.experimental import pallas as pl
from jax.experimental.pallas import tpu as pltpu
from jax.sharding import PartitionSpec as P

LANES = 128
GROUP = 4
CHUNKS = 2
RING = 4
EDGE = 16
MESH = pl.DeviceIdType.MESH
F32 = jnp.float32
BF16 = jnp.bfloat16


def half_table(size):
    half = size // 2
    rows = np.arange(half, dtype=np.int64)[:, None]
    cols = np.arange(size, dtype=np.int64)[None, :]
    freq = np.where(cols < half, cols, cols - half)
    angle = (rows * freq % size).astype(np.float64) * (2.0 * np.pi / size)
    nyquist = np.where(rows % 2 == 0, 1.0, -1.0)
    table = np.where(cols < half, np.cos(angle), np.where(cols == half, nyquist, -np.sin(angle)))
    return table.astype(ml_dtypes.bfloat16)


def rows_of(ref):
    blocks, chans, width = ref.shape
    return ref[...].astype(F32).reshape(blocks * chans, width).astype(BF16)


def source_spectra(x_ref, table, xs):
    blocks, chans, half = x_ref.shape
    spec = jnp.dot(rows_of(x_ref), table[...], preferred_element_type=F32)
    for part in range(2):
        for q in range(half // LANES):
            at = part * half + q * LANES
            xs[part, q] = spec[:, at : at + LANES].reshape(blocks, chans, LANES)


def filter_spectra(h_ref, table, hs):
    blocks, chans, half = h_ref.shape
    size = 2 * half
    lead = GROUP - 1
    filt = jnp.dot(rows_of(h_ref), table[...], preferred_element_type=F32)
    lane = lax.broadcasted_iota(jnp.int32, (1, 1, LANES), 2)
    for q in range(half // LANES):
        inside = (lane > 0) if q == 0 else (lane >= 0)
        weight = jnp.where(inside, 2.0 / size, 1.0 / size).astype(F32)
        signed = jnp.where(lane % 2 == 0, weight, -weight)
        parts = []
        for part in range(2):
            at = part * half + q * LANES
            block = filt[:, at : at + LANES].reshape(blocks, chans, LANES)
            before = jnp.concatenate(
                [jnp.zeros((1, chans, LANES), F32), block[: blocks - 1]], axis=0
            )
            parts.append(before * signed + block * weight)
        real, imag = parts
        keep = jnp.broadcast_to(inside, real.shape)
        hs[0, q, lead:] = real
        hs[1, q, lead:] = jnp.where(keep, imag, 0.0)
        hs[2, q, lead:] = jnp.where(keep, real, imag)
        for kind in range(3):
            hs[kind, q, :lead] = jnp.zeros((lead, chans, LANES), F32)


def block_products(xs, hs, low):
    _, tiles, blocks, chans, _ = xs.shape
    half = tiles * LANES
    lead = GROUP - 1

    def one_tile(q, _):
        def one_group(big, _):
            def one_source(small, total):
                gap = big - small
                xr = [xs[0, q, GROUP * small + b] for b in range(GROUP)]
                xi = [xs[1, q, GROUP * small + b] for b in range(GROUP)]
                gr, gi, g2 = (
                    [hs[kind, q, GROUP * gap + m] for m in range(2 * GROUP - 1)]
                    for kind in range(3)
                )
                total = list(total)
                for a in range(GROUP):
                    for b in range(GROUP):
                        m = a - b + lead
                        total[a] += xr[b] * gr[m] - xi[b] * gi[m]
                        total[GROUP + a] += xr[b] * gi[m] + xi[b] * g2[m]
                return tuple(total)

            zero = jnp.zeros((chans, LANES), F32)
            total = lax.fori_loop(0, big + 1, one_source, (zero,) * (2 * GROUP))
            rows = pl.ds(pl.multiple_of(big * GROUP * chans, GROUP * chans), GROUP * chans)
            for part in range(2):
                cols = pl.ds(pl.multiple_of(part * half + q * LANES, LANES), LANES)
                piece = jnp.concatenate(total[part * GROUP : (part + 1) * GROUP], axis=0)
                low[rows, cols] = piece.astype(BF16)
            return 0

        return lax.fori_loop(0, blocks // GROUP, one_group, 0)

    lax.fori_loop(0, tiles, one_tile, 0)


def take(sem, ref):
    pltpu.make_async_copy(ref, ref, sem).wait()


def operator_kernel(
    n_ctx,
    n_ch,
    streams,
    taps_in,
    filters,
    skip_in,
    table_in,
    weight,
    out,
    strm,
    taps,
    filt,
    skip,
    table,
    wide,
    pad,
    halo,
    send_h,
    recv_h,
    send_x,
    recv_x,
    send_y,
    recv_y,
    xs,
    hs,
    low,
    outer,
    direct,
    gat,
    acc,
    out_v,
    local_sem,
    halo_sem,
    h_sem,
    x_sem,
    y_sem,
    w_sem,
    f_sem,
    g_send,
    g_recv,
    out_sem,
):
    me = lax.axis_index("ctx")
    col = lax.axis_index("ch")
    core = lax.rem(me, 2)
    partner = me + 1 - 2 * core
    _, seg, chans = streams.shape
    share = chans // n_ctx
    cols = weight.shape[1] // n_ch
    rows = chans // 2
    step = seg // CHUNKS

    own_cols = pl.ds(pl.multiple_of(col * cols, cols), cols)
    loads = [
        pltpu.make_async_copy(filters, filt, local_sem.at[0]),
        pltpu.make_async_copy(streams, strm, local_sem.at[1]),
        pltpu.make_async_copy(taps_in, taps, local_sem.at[2]),
        pltpu.make_async_copy(skip_in, skip, local_sem.at[3]),
        pltpu.make_async_copy(table_in, table, local_sem.at[4]),
        pltpu.make_async_copy(weight.at[:, own_cols], wide.at[col], local_sem.at[5]),
    ]
    for load in loads:
        load.start()

    barrier = pltpu.get_barrier_semaphore()

    def greet_ctx(k, _):
        pl.semaphore_signal(
            barrier, inc=1, device_id={"ctx": lax.rem(me + k, n_ctx)}, device_id_type=MESH
        )
        return 0

    def greet_ch(k, _):
        pl.semaphore_signal(
            barrier, inc=1, device_id={"ch": lax.rem(col + k, n_ch)}, device_id_type=MESH
        )
        return 0

    lax.fori_loop(1, n_ctx, greet_ctx, 0)
    lax.fori_loop(1, n_ch, greet_ch, 0)

    loads[0].wait()
    send_h[...] = filt[...].astype(F32).T.reshape(n_ctx, share, seg).astype(BF16)
    recv_h[me] = send_h[me]
    pl.semaphore_wait(barrier, n_ctx - 1 + n_ch - 1)

    edge = pltpu.make_async_remote_copy(
        src_ref=streams.at[:, pl.ds(seg - EDGE, EDGE), :],
        dst_ref=halo,
        send_sem=halo_sem.at[0],
        recv_sem=halo_sem.at[1],
        device_id={"ctx": lax.rem(me + 1, n_ctx)},
        device_id_type=MESH,
    )
    edge.start()

    def exchange(source, target, sem):
        def one(k, _):
            reach = lax.div(k + 1, 2)
            there = lax.rem(me + jnp.where(lax.rem(k, 2) == 1, reach, n_ctx - reach), n_ctx)
            pltpu.make_async_remote_copy(
                src_ref=source.at[there],
                dst_ref=target.at[me],
                send_sem=sem.at[0],
                recv_sem=sem.at[1],
                device_id={"ctx": there},
                device_id_type=MESH,
            ).start()
            return 0

        lax.fori_loop(1, n_ctx, one, 0)

    exchange(send_h, recv_h, h_sem)

    loads[1].wait()
    loads[2].wait()
    loads[3].wait()
    for q in range(3):
        pad[q, 8:] = strm[q].astype(F32)
    edge.wait_recv()
    pad[:, :8] = jnp.where(me > 0, halo[...].astype(F32)[:, EDGE - 8 :], 0.0)
    piece = min(LANES, seg)
    for at in range(0, seg, piece):

        def mixed(q):
            total = taps[0, q : q + 1] * pad[q, 8 + at : 8 + at + piece]
            total = total + taps[1, q : q + 1] * pad[q, 7 + at : 7 + at + piece]
            return total + taps[2, q : q + 1] * pad[q, 6 + at : 6 + at + piece]

        inner = (mixed(0) * mixed(1)).astype(BF16).astype(F32)
        send_x[:, :, at : at + piece] = inner.T.reshape(n_ctx, share, piece).astype(BF16)
        direct[at : at + piece] = skip[...] * inner
        outer[at : at + piece] = mixed(2)
    recv_x[me] = send_x[me]
    exchange(send_x, recv_x, x_sem)

    half_rows = pl.ds(pl.multiple_of(core * rows, rows), rows)

    def lend(k, _):
        there = lax.rem(col + k, n_ch)
        pltpu.make_async_remote_copy(
            src_ref=weight.at[half_rows, pl.ds(pl.multiple_of(there * cols, cols), cols)],
            dst_ref=wide.at[col, half_rows],
            send_sem=w_sem.at[0],
            recv_sem=w_sem.at[1],
            device_id={"ch": there},
            device_id_type=MESH,
        ).start()
        return 0

    lax.fori_loop(1, n_ch, lend, 0)

    loads[4].wait()
    others = pl.ds(0, n_ctx - 1)
    take(h_sem.at[1], recv_h.at[others])
    filter_spectra(recv_h, table, hs)
    take(x_sem.at[1], recv_x.at[others])
    source_spectra(recv_x, table, xs)
    block_products(xs, hs, low)
    for kk in range(CHUNKS):
        part = lax.dot_general(
            low[...],
            table[kk * step : (kk + 1) * step],
            (((1,), (1,)), ((), ())),
            preferred_element_type=F32,
        )
        send_y[kk] = part.reshape(n_ctx, share, step).astype(BF16)
        recv_y[kk, me] = send_y[kk, me]
        exchange(send_y.at[kk], recv_y.at[kk], y_sem.at[kk])

    base = RING * lax.div(col, RING)
    place = lax.rem(col, RING)
    right = base + lax.rem(place + 1, RING)
    left = base + lax.rem(place + RING - 1, RING)
    far = base + lax.rem(place + 2, RING)
    swap = RING - 2 * base
    across, a_left, a_right, a_far = (c + swap for c in (col, left, right, far))
    full, first, second = pl.ds(0, step), pl.ds(0, step // 2), pl.ds(step // 2, step // 2)

    def hop(kk, kind, block, span, there):
        return pltpu.make_async_remote_copy(
            src_ref=gat.at[block, kk, span],
            dst_ref=gat.at[block, kk, span],
            send_sem=g_send.at[kk, kind],
            recv_sem=g_recv.at[kk, kind],
            device_id={"ch": there},
            device_id_type=MESH,
        )

    sent = []

    def push(*what):
        copy = hop(*what)
        copy.start()
        sent.append(copy)

    def arrived(kk, kind, block, span):
        hop(kk, kind, block, span, across).wait_recv()

    forward = []
    for kk in range(CHUNKS):
        take(y_sem.at[kk, 1], recv_y.at[kk, others])
        conv = recv_y[kk].astype(F32).reshape(chans, step).T
        at = kk * step
        gated = outer[at : at + step] * (conv + direct[at : at + step])
        gat[col, kk] = gated.astype(BF16)
        push(kk, 0, col, full, right)
        push(kk, 1, col, full, left)
        push(kk, 2, col, full, across)
    take(w_sem.at[1], wide.at[pl.ds(0, n_ch - 1), pl.ds(0, rows)])

    def pass_on(k, _):
        block = lax.rem(col + k, n_ch)
        pltpu.make_async_remote_copy(
            src_ref=wide.at[block, half_rows],
            dst_ref=wide.at[block, half_rows],
            send_sem=f_sem.at[0],
            recv_sem=f_sem.at[1],
            device_id={"ctx": partner},
            device_id_type=MESH,
        ).start()
        return 0

    lax.fori_loop(1, n_ch, pass_on, 0)

    for kk in range(CHUNKS):
        arrived(kk, 0, left, full)
        push(kk, 3, left, first, right)
        arrived(kk, 1, right, full)
        push(kk, 4, right, second, left)
        arrived(kk, 2, across, full)
        push(kk, 5, across, full, right)
        push(kk, 6, across, full, left)
    for kk in range(CHUNKS):
        arrived(kk, 3, far, first)
        arrived(kk, 4, far, second)
        push(kk, 7, far, full, across)
    loads[5].wait()
    take(f_sem.at[1], wide.at[pl.ds(0, n_ch - 1), pl.ds(0, rows)])

    def product(block, kk):
        return jnp.dot(gat[block, kk], wide[block], preferred_element_type=F32)

    for kk in range(CHUNKS):
        near = product(col, kk) + product(left, kk)
        acc[kk] = near + (product(right, kk) + product(across, kk)) + product(far, kk)
    for kk in range(CHUNKS):
        arrived(kk, 5, a_left, full)
        arrived(kk, 6, a_right, full)
        acc[kk] += product(a_left, kk) + product(a_right, kk)
    stores = []
    for kk in range(CHUNKS):
        arrived(kk, 7, a_far, full)
        span = pl.ds(kk * step, step)
        out_v[span] = (acc[kk] + product(a_far, kk)).astype(BF16)
        stores.append(pltpu.make_async_copy(out_v.at[span], out.at[span], out_sem.at[kk]))
        stores[-1].start()

    edge.wait_send()
    take(h_sem.at[0], send_h.at[others])
    take(x_sem.at[0], send_x.at[others])
    for kk in range(CHUNKS):
        take(y_sem.at[kk, 0], send_y.at[kk, others])
    take(w_sem.at[0], wide.at[pl.ds(0, n_ch - 1), pl.ds(0, rows)])
    take(f_sem.at[0], wide.at[pl.ds(0, n_ch - 1), pl.ds(0, rows)])
    for copy in sent:
        copy.wait_send()
    for store in stores:
        store.wait()


def local(streams, short_taps, filters, skip_gain, out_weight, *, table):
    n_ctx, n_ch = lax.axis_size("ctx"), lax.axis_size("ch")
    seg, _, chans = streams.shape
    share = chans // n_ctx
    cols = out_weight.shape[1] // n_ch
    tiles = seg // LANES
    step = seg // CHUNKS
    slabs = pltpu.VMEM((n_ctx, share, seg), BF16)
    pieces = pltpu.VMEM((CHUNKS, n_ctx, share, step), BF16)
    dma = pltpu.SemaphoreType.DMA
    return pl.pallas_call(
        functools.partial(operator_kernel, n_ctx, n_ch),
        out_shape=jax.ShapeDtypeStruct((seg, cols), BF16),
        in_specs=[pl.BlockSpec(memory_space=pl.ANY)] * 6,
        out_specs=pl.BlockSpec(memory_space=pl.ANY),
        scratch_shapes=[
            pltpu.VMEM((3, seg, chans), BF16),
            pltpu.VMEM(short_taps.shape, F32),
            pltpu.VMEM((seg, chans), BF16),
            pltpu.VMEM((1, chans), F32),
            pltpu.VMEM((seg, 2 * seg), BF16),
            pltpu.VMEM((n_ch, chans, cols), BF16),
            pltpu.VMEM((3, seg + 8, chans), F32),
            pltpu.VMEM((3, EDGE, chans), BF16),
            slabs,
            slabs,
            slabs,
            slabs,
            pieces,
            pieces,
            pltpu.VMEM((2, tiles, n_ctx, share, LANES), F32),
            pltpu.VMEM((3, tiles, n_ctx + GROUP - 1, share, LANES), F32),
            pltpu.VMEM((n_ctx * share, 2 * seg), BF16),
            pltpu.VMEM((seg, chans), F32),
            pltpu.VMEM((seg, chans), F32),
            pltpu.VMEM((n_ch, CHUNKS, step, chans), BF16),
            pltpu.VMEM((CHUNKS, step, cols), F32),
            pltpu.VMEM((seg, cols), BF16),
            dma((6,)),
            dma((2,)),
            dma((2,)),
            dma((2,)),
            dma((CHUNKS, 2)),
            dma((2,)),
            dma((2,)),
            dma((CHUNKS, 8)),
            dma((CHUNKS, 8)),
            dma((CHUNKS,)),
        ],
        compiler_params=pltpu.CompilerParams(
            collective_id=0, has_side_effects=True, vmem_limit_bytes=48 << 20
        ),
        name="hyena_operator",
    )(
        jnp.transpose(streams, (1, 0, 2)),
        short_taps,
        filters,
        skip_gain[None],
        table,
        out_weight,
    )


def solution(mesh):
    seg = 16384 // mesh.shape["ctx"]
    return jax.shard_map(
        functools.partial(local, table=half_table(2 * seg)),
        mesh=mesh,
        in_specs=(
            P("ctx", None, "ch"),
            P(None, None, "ch"),
            P("ctx", "ch"),
            P("ch"),
            P("ch", None),
        ),
        out_specs=P("ctx", "ch"),
        check_vma=False,
    )
```

time: 141 us -> 67.6 us (0.48)
  the two profiles are of different devices: /device:TPU:18 before, /device:TPU:1 now
where the time goes in v2:
time: 67.6 us; the launch traced here: 67.2 us
  Pallas kernels  60.1 us (89%)
  local copies, waits for them, and re-layouts  7.08 us (10%)
    pallas_call x1, Pallas kernels, local(): pl.pallas_call(functools.partial(operator_kernel, n_ctx, n_ch), out_shape...  60.1 us
    unnamed x13, local copies, waits for them, and re-layouts  7.08 us

profile of v2, /device:TPU:1, one launch (start us, length us, event | category | flops | bytes accessed | tf_op | source)
XLA Modules:
  0.0 67.2 jit_solution(8464778350058483190)
XLA Ops:
  0.0 0.0 copy-start
  0.0 1.6 %copy-done = bf16[256,4096]{1,0:T(8,128)(2,1)S(1)} copy-done((bf16[256,4096]{1,0:T(8,128)(2,1)S(1)}, bf16[256,4096]{1,0:T(8,128)(2,1)}, u32[]{:S(2)}) %copy-start) | copy-done | bytes 2097176
  1.6 0.0 copy-start.1
  1.6 1.2 %copy-done.1 = bf16[512,1024]{1,0:T(8,128)(2,1)S(1)} copy-done((bf16[512,1024]{1,0:T(8,128)(2,1)S(1)}, bf16[512,1024]{1,0:T(8,128)(2,1)}, u32[]{:S(2)}) %copy-start.1) | copy-done | bytes 1048600
  2.8 0.0 copy-start.2
  2.8 1.1 %copy-done.2 = bf16[512,3,256]{2,0,1:T(8,128)(2,1)S(1)} copy-done((bf16[512,3,256]{2,0,1:T(8,128)(2,1)S(1)}, bf16[512,3,256]{2,0,1:T(8,128)(2,1)}, u32[]{:S(2)}) %copy-start.2) | copy-done | bytes 786456
  4.0 0.0 copy-start.3
  4.0 0.9 %copy-done.3 = bf16[512,256]{1,0:T(8,128)(2,1)S(1)} copy-done((bf16[512,256]{1,0:T(8,128)(2,1)S(1)}, bf16[512,256]{1,0:T(8,128)(2,1)}, u32[]{:S(2)}) %copy-start.3) | copy-done | bytes 262168
  4.9 0.0 copy-start.4
  4.9 0.7 %copy-done.4 = f32[3,3,256]{2,1,0:T(4,128)S(1)} copy-done((f32[3,3,256]{2,1,0:T(4,128)S(1)}, f32[3,3,256]{2,1,0:T(4,128)}, u32[]{:S(2)}) %copy-start.4) | copy-done | bytes 9240
  5.6 0.0 copy-start.5
  5.6 0.7 %copy-done.5 = f32[256]{0:T(256)S(1)} copy-done((f32[256]{0:T(256)S(1)}, f32[256]{0:T(256)}, u32[]{:S(2)}) %copy-start.5) | copy-done | bytes 1048
  6.3 60.1 %hyena_operator.1 = bf16[512,512]{1,0:T(8,128)(2,1)S(1)} custom-call(bf16[3,512,256]{2,1,0:T(8,128)(2,1)S(1)} %bitcast.2, f32[3,3,256]{2,1,0:T(4,128)S(1)} %copy-done.4, bf16[512,256]{1,0:T(8,128)(2,1)S(1)} %copy-done.3, f32[1,256]{1,0:T(1,128)S(1)} %bitcast.3, bf16[512,1024]{1,0:T(8,128)(2,1)S(1)} %copy-done.1, bf16[256,4096]{1,0:T(8,128)(2,1)S(1)} %copy-done), custom_call_target="tpu_custom_call" | custom-call | tf_op jit(solution)/shard_map/hyena_operator/pallas_call | solution.py:397
  66.4 0.8 %copy.8 = bf16[512,512]{1,0:T(8,128)(2,1)} copy(bf16[512,512]{1,0:T(8,128)(2,1)S(1)} %hyena_operator.1) | data formatting | bytes 1048576
Async XLA Ops:
  0.0 1.6 %copy-start = (bf16[256,4096]{1,0:T(8,128)(2,1)S(1)}, bf16[256,4096]{1,0:T(8,128)(2,1)}, u32[]{:S(2)}) copy-start(bf16[256,4096]{1,0:T(8,128)(2,1)} %weight.1) | copy-start | bytes 6291460
  1.6 1.2 %copy-start.1 = (bf16[512,1024]{1,0:T(8,128)(2,1)S(1)}, bf16[512,1024]{1,0:T(8,128)(2,1)}, u32[]{:S(2)}) copy-start(bf16[512,1024]{1,0:T(8,128)(2,1)} %constant.2.clone.table_in) | copy-start | bytes 3145732
  2.8 1.1 %copy-start.2 = (bf16[512,3,256]{2,0,1:T(8,128)(2,1)S(1)}, bf16[512,3,256]{2,0,1:T(8,128)(2,1)}, u32[]{:S(2)}) copy-start(bf16[512,3,256]{2,0,1:T(8,128)(2,1)} %param.6) | copy-start | bytes 2359300
  4.0 0.9 %copy-start.3 = (bf16[512,256]{1,0:T(8,128)(2,1)S(1)}, bf16[512,256]{1,0:T(8,128)(2,1)}, u32[]{:S(2)}) copy-start(bf16[512,256]{1,0:T(8,128)(2,1)} %filters.1) | copy-start | bytes 786436
  4.9 0.7 %copy-start.4 = (f32[3,3,256]{2,1,0:T(4,128)S(1)}, f32[3,3,256]{2,1,0:T(4,128)}, u32[]{:S(2)}) copy-start(f32[3,3,256]{2,1,0:T(4,128)} %taps_in.1) | copy-start | bytes 27652
  5.6 0.7 %copy-start.5 = (f32[256]{0:T(256)S(1)}, f32[256]{0:T(256)}, u32[]{:S(2)}) copy-start(f32[256]{0:T(256)} %param.9) | copy-start | bytes 3076

commit v3 on v2

--- a/solution.py
+++ b/solution.py
@@ -434,7 +434,7 @@
             dma((CHUNKS,)),
         ],
         compiler_params=pltpu.CompilerParams(
-            collective_id=0, has_side_effects=True, vmem_limit_bytes=48 << 20
+            collective_id=0, has_side_effects=True, vmem_limit_bytes=67043328
         ),
         name="hyena_operator",
     )(

time: 67.6 us -> 63.6 us (0.941)
  local copies, waits for them, and re-layouts: 7.08 us -> 1.87 us
  Pallas kernels: 60.1 us -> 61.4 us
    unnamed x13 -> x1, local copies, waits for them, and re-layouts: 7.08 us -> 1.87 us
    pallas_call x1, Pallas kernels: 60.1 us -> 61.4 us  [local(): pl.pallas_call(functools.partial(operator_kernel, n_ctx, n_ch), out_shape...]
where the time goes in v3:
time: 63.6 us; the launch traced here: 63.3 us
  Pallas kernels  61.4 us (97%)
  local copies, waits for them, and re-layouts  1.87 us (3%)
    pallas_call x1, Pallas kernels, local(): pl.pallas_call(functools.partial(operator_kernel, n_ctx, n_ch), out_shape...  61.4 us
    unnamed x1, local copies, waits for them, and re-layouts  1.87 us

profile of v3, /device:TPU:1, one launch (start us, length us, event | category | flops | bytes accessed | tf_op | source)
XLA Modules:
  0.0 63.3 jit_solution(2488068579580508765)
XLA Ops:
  0.0 61.4 %hyena_operator.1 = bf16[512,512]{1,0:T(8,128)(2,1)} custom-call(bf16[3,512,256]{2,1,0:T(8,128)(2,1)} %bitcast.2, f32[3,3,256]{2,1,0:T(4,128)} %taps_in.1, bf16[512,256]{1,0:T(8,128)(2,1)} %filters.1, f32[1,256]{1,0:T(1,128)} %bitcast.3, bf16[512,1024]{1,0:T(8,128)(2,1)} %constant.2.clone.table_in, bf16[256,4096]{1,0:T(8,128)(2,1)} %weight.1), custom_call_target="tpu_custom_call" | custom-call | tf_op jit(solution)/shard_map/hyena_operator/pallas_call | solution.py:397
  61.4 1.9 %copy.8 = bf16[512,512]{1,0:T(8,128)(2,1)} copy(bf16[512,512]{1,0:T(8,128)(2,1)} %hyena_operator.1) | data formatting | bytes 1048576

commit v4 on v3

v4 whole, which is shorter than its diff:
```python
import functools

import jax
import jax.numpy as jnp
import ml_dtypes
import numpy as np
from jax import lax
from jax.experimental import pallas as pl
from jax.experimental.pallas import tpu as pltpu
from jax.sharding import PartitionSpec as P

LANES = 128
GROUP = 4
SPLITS = (1, 1, 1, 1)
HALVES = 2
LEAD = 2 * GROUP - 1
RING = 4
EDGE = 16
MESH = pl.DeviceIdType.MESH
F32 = jnp.float32
BF16 = jnp.bfloat16


def half_table(size):
    half = size // 2
    rows = np.arange(half, dtype=np.int64)[:, None]
    cols = np.arange(size, dtype=np.int64)[None, :]
    freq = np.where(cols < half, cols, cols - half)
    angle = (rows * freq % size).astype(np.float64) * (2.0 * np.pi / size)
    nyquist = np.where(rows % 2 == 0, 1.0, -1.0)
    table = np.where(cols < half, np.cos(angle), np.where(cols == half, nyquist, -np.sin(angle)))
    return table.astype(ml_dtypes.bfloat16)


def rows_of(ref):
    blocks, chans, width = ref.shape
    return ref[...].astype(F32).reshape(blocks * chans, width).astype(BF16)


def source_spectra(x_ref, table, xs):
    blocks, chans, half = x_ref.shape
    spec = jnp.dot(rows_of(x_ref), table[...], preferred_element_type=F32)
    lane = lax.broadcasted_iota(jnp.int32, (1, 1, LANES), 2)
    for q in range(half // LANES):
        real, imag = (
            spec[:, at : at + LANES].reshape(blocks, chans, LANES)
            for at in (q * LANES, half + q * LANES)
        )
        xs[0, q] = real + imag
        if q == 0:
            inside = jnp.broadcast_to(lane > 0, real.shape)
            real, imag = jnp.where(inside, real, imag), jnp.where(inside, imag, real)
        xs[1, q] = real
        xs[2, q] = imag


def filter_spectra(h_ref, table, hs):
    blocks, chans, half = h_ref.shape
    size = 2 * half
    filt = jnp.dot(rows_of(h_ref), table[...], preferred_element_type=F32)
    lane = lax.broadcasted_iota(jnp.int32, (1, 1, LANES), 2)
    for q in range(half // LANES):
        inside = (lane > 0) if q == 0 else (lane >= 0)
        weight = jnp.where(inside, 2.0 / size, 1.0 / size).astype(F32)
        signed = jnp.where(lane % 2 == 0, weight, -weight)
        parts = []
        for part in range(2):
            at = part * half + q * LANES
            block = filt[:, at : at + LANES].reshape(blocks, chans, LANES)
            before = jnp.concatenate(
                [jnp.zeros((1, chans, LANES), F32), block[: blocks - 1]], axis=0
            )
            parts.append(before * signed + block * weight)
        real, imag = parts
        terms = (real, imag - real, imag + real)
        if q == 0:
            keep = jnp.broadcast_to(inside, real.shape)
            lone = (0.0, imag, -real)
            terms = tuple(jnp.where(keep, t, e) for t, e in zip(terms, lone, strict=True))
        for kind in range(3):
            hs[kind, q, LEAD:] = terms[kind]
            hs[kind, q, :LEAD] = jnp.zeros((LEAD, chans, LANES), F32)


def block_products(parity, xs, hs, low):
    _, tiles, blocks, chans, _ = xs.shape
    half = tiles * LANES

    def one_tile(q, _):
        def one_group(big, _):
            def one_source(small, total):
                total = list(total)
                for b in range(2):
                    gap = 2 * GROUP * (big - small) + 1 + parity - b
                    for kind in range(3):
                        x = [xs[kind, q, 2 * (GROUP * small + j) + b] for j in range(GROUP)]
                        g = [hs[kind, q, gap + 2 * m] for m in range(2 * GROUP - 1)]
                        for i in range(GROUP):
                            for j in range(GROUP):
                                total[kind * GROUP + i] += x[j] * g[i - j + GROUP - 1]
                return tuple(total)

            zero = jnp.zeros((chans, LANES), F32)
            total = lax.fori_loop(0, big + 1, one_source, (zero,) * (3 * GROUP))
            rows = pl.ds(pl.multiple_of(big * GROUP * chans, GROUP * chans), GROUP * chans)
            both, second, third = (total[k * GROUP : (k + 1) * GROUP] for k in range(3))
            real = [p - r for p, r in zip(both, third, strict=True)]
            imag = [p + r for p, r in zip(both, second, strict=True)]
            for part, value in enumerate((real, imag)):
                cols = pl.ds(pl.multiple_of(part * half + q * LANES, LANES), LANES)
                low[parity, rows, cols] = jnp.concatenate(value, axis=0).astype(BF16)
            return 0

        return lax.fori_loop(0, blocks // (2 * GROUP), one_group, 0)

    lax.fori_loop(0, tiles, one_tile, 0)


def take(sem, ref):
    pltpu.make_async_copy(ref, ref, sem).wait()


def operator_kernel(
    n_ctx,
    n_ch,
    streams,
    taps_in,
    filters,
    skip_in,
    table_in,
    weight,
    out,
    strm,
    taps,
    filt,
    skip,
    table,
    wide,
    pad,
    halo,
    send_h,
    recv_h,
    send_x,
    recv_x,
    send_y,
    recv_y,
    xs,
    hs,
    low,
    outer,
    direct,
    gat,
    give,
    gain,
    acc,
    out_v,
    local_sem,
    halo_sem,
    h_sem,
    x_sem,
    y_sem,
    w_sem,
    f_sem,
    g_send,
    g_recv,
    p_sem,
    out_sem,
):
    me = lax.axis_index("ctx")
    col = lax.axis_index("ch")
    core = lax.rem(me, 2)
    partner = me + 1 - 2 * core
    _, seg, chans = streams.shape
    share = chans // n_ctx
    cols = weight.shape[1] // n_ch
    rows = chans // 2

    base = RING * lax.div(col, RING)
    place = lax.rem(col, RING)
    r_place, l_place, f_place = (lax.rem(place + d, RING) for d in (1, RING - 1, 2))
    right, left = base + r_place, base + l_place
    across = col + RING - 2 * base

    def columns(block):
        return pl.ds(pl.multiple_of(block * cols, cols), cols)

    loads = [
        pltpu.make_async_copy(filters, filt, local_sem.at[0]),
        pltpu.make_async_copy(streams, strm, local_sem.at[1]),
        pltpu.make_async_copy(taps_in, taps, local_sem.at[2]),
        pltpu.make_async_copy(skip_in, skip, local_sem.at[3]),
        pltpu.make_async_copy(table_in, table, local_sem.at[4]),
        pltpu.make_async_copy(weight.at[:, columns(col)], wide.at[place, 0], local_sem.at[5]),
        pltpu.make_async_copy(weight.at[:, columns(across)], wide.at[place, 1], local_sem.at[6]),
    ]
    for load in loads:
        load.start()

    barrier = pltpu.get_barrier_semaphore()

    def greet_ctx(k, _):
        pl.semaphore_signal(
            barrier, inc=1, device_id={"ctx": lax.rem(me + k, n_ctx)}, device_id_type=MESH
        )
        return 0

    def greet_ch(k, _):
        pl.semaphore_signal(
            barrier, inc=1, device_id={"ch": lax.rem(col + k, n_ch)}, device_id_type=MESH
        )
        return 0

    lax.fori_loop(1, n_ctx, greet_ctx, 0)
    lax.fori_loop(1, n_ch, greet_ch, 0)

    piece = min(LANES, seg)

    def mix(at):
        def mixed(q):
            total = taps[0, q : q + 1] * pad[q, 8 + at : 8 + at + piece]
            total = total + taps[1, q : q + 1] * pad[q, 7 + at : 7 + at + piece]
            return total + taps[2, q : q + 1] * pad[q, 6 + at : 6 + at + piece]

        inner = (mixed(0) * mixed(1)).astype(BF16).astype(F32)
        send_x[:, :, at : at + piece] = inner.T.reshape(n_ctx, share, piece).astype(BF16)
        direct[at : at + piece] = skip[...] * inner
        outer[at : at + piece] = mixed(2)

    loads[0].wait()
    send_h[...] = filt[...].astype(F32).T.reshape(n_ctx, share, seg).astype(BF16)
    recv_h[me] = send_h[me]
    for load in loads[1:4]:
        load.wait()
    for q in range(3):
        pad[q, 8:] = strm[q].astype(F32)
    for at in range(piece, seg, piece):
        mix(at)
    pl.semaphore_wait(barrier, n_ctx - 1 + n_ch - 1)

    edge = pltpu.make_async_remote_copy(
        src_ref=streams.at[:, pl.ds(seg - EDGE, EDGE), :],
        dst_ref=halo,
        send_sem=halo_sem.at[0],
        recv_sem=halo_sem.at[1],
        device_id={"ctx": lax.rem(me + 1, n_ctx)},
        device_id_type=MESH,
    )
    edge.start()

    def slab(source, target, sem, there):
        pltpu.make_async_remote_copy(
            src_ref=source,
            dst_ref=target.at[me],
            send_sem=sem.at[0],
            recv_sem=sem.at[1],
            device_id={"ctx": there},
            device_id_type=MESH,
        ).start()

    def exchange(source, target, sem):
        def one(k, _):
            reach = lax.div(k + 1, 2)
            there = lax.rem(me + jnp.where(lax.rem(k, 2) == 1, reach, n_ctx - reach), n_ctx)
            slab(source.at[there], target, sem, there)
            return 0

        lax.fori_loop(1, n_ctx, one, 0)

    exchange(send_h, recv_h, h_sem)
    edge.wait_recv()
    pad[:, :8] = jnp.where(me > 0, halo[...].astype(F32)[:, EDGE - 8 :], 0.0)
    mix(0)
    recv_x[me] = send_x[me]
    exchange(send_x, recv_x, x_sem)

    half_rows = pl.ds(pl.multiple_of(core * rows, rows), rows)

    def lend(k, _):
        there = lax.rem(place + k, RING)
        for side, block in enumerate((base + there, across - place + there)):
            pltpu.make_async_remote_copy(
                src_ref=weight.at[half_rows, columns(block)],
                dst_ref=wide.at[place, side, half_rows],
                send_sem=w_sem.at[0],
                recv_sem=w_sem.at[1],
                device_id={"ch": base + there},
                device_id_type=MESH,
            ).start()
        return 0

    lax.fori_loop(1, RING, lend, 0)

    loads[4].wait()
    others = pl.ds(0, n_ctx - 1)
    take(h_sem.at[1], recv_h.at[others])
    filter_spectra(recv_h, table, hs)
    take(x_sem.at[1], recv_x.at[others])
    source_spectra(recv_x, table, xs)
    pairs = n_ctx // 2
    mine = lax.div(me, 2)
    wing = seg // HALVES
    for parity in range(2):
        block_products(parity, xs, hs, low)
        for side in range(HALVES):
            part = lax.dot_general(
                low[parity],
                table[side * wing : (side + 1) * wing],
                (((1,), (1,)), ((), ())),
                preferred_element_type=F32,
            )
            send_y[side, parity] = part.reshape(pairs, share, wing).astype(BF16)

            def back(k, _, side=side, parity=parity):
                reach = lax.div(k + 1, 2)
                pair = lax.rem(mine + jnp.where(lax.rem(k, 2) == 1, reach, pairs - reach), pairs)
                there = 2 * pair + parity

                @pl.when(there != me)
                def _():
                    slab(
                        send_y.at[side, parity, pair], recv_y.at[side], y_sem.at[side], there
                    )

                return 0

            lax.fori_loop(0, pairs, back, 0)
    for side in range(HALVES):
        recv_y[side, me] = send_y[side, core, mine]

    lent = wide.at[pl.ds(0, RING - 1), :, pl.ds(0, rows)]
    take(w_sem.at[1], lent)

    def pass_on(k, _):
        there = lax.rem(place + k, RING)
        pltpu.make_async_remote_copy(
            src_ref=wide.at[there, :, half_rows],
            dst_ref=wide.at[there, :, half_rows],
            send_sem=f_sem.at[0],
            recv_sem=f_sem.at[1],
            device_id={"ctx": partner},
            device_id_type=MESH,
        ).start()
        return 0

    lax.fori_loop(1, RING, pass_on, 0)

    unit = seg // sum(SPLITS)
    starts = [unit * sum(SPLITS[:kk]) for kk in range(len(SPLITS))]
    sizes = [unit * split for split in SPLITS]
    last = len(SPLITS) - 1
    full = [pl.ds(at, size) for at, size in zip(starts, sizes, strict=True)]
    first = [pl.ds(at, size // 2) for at, size in zip(starts, sizes, strict=True)]
    second = [pl.ds(at + size // 2, size // 2) for at, size in zip(starts, sizes, strict=True)]

    def hop(kk, kind, block, spans, there):
        span = spans[kk]
        return pltpu.make_async_remote_copy(
            src_ref=gat.at[block, span],
            dst_ref=gat.at[block, span],
            send_sem=g_send.at[kk, kind],
            recv_sem=g_recv.at[kk, kind],
            device_id={"ch": there},
            device_id_type=MESH,
        )

    sent = []

    def push(copy):
        copy.start()
        sent.append(copy)

    def begin(kk):
        at, size = starts[kk], sizes[kk]
        side, inside = at // wing, at % wing
        if inside == 0:
            take(y_sem.at[side, 1], recv_y.at[side, others])
        conv = recv_y[side, :, :, inside : inside + size].astype(F32).reshape(chans, size).T
        gated = outer[full[kk]] * (conv + direct[full[kk]])
        gat[place, full[kk]] = gated.astype(BF16)
        push(hop(kk, 0, place, full, right))
        push(hop(kk, 1, place, full, left))
        push(hop(kk, 2, place, full, base + f_place))

    def relay(kk):
        hop(kk, 0, l_place, full, left).wait_recv()
        hop(kk, 1, r_place, full, right).wait_recv()

    def partial(kk, side):
        total = jnp.dot(gat[place, full[kk]], wide[place, side], preferred_element_type=F32)
        for block in (l_place, r_place, f_place):
            total += jnp.dot(gat[block, full[kk]], wide[block, side], preferred_element_type=F32)
        return total

    def share_out(kk):
        return pltpu.make_async_remote_copy(
            src_ref=give.at[full[kk]],
            dst_ref=gain.at[full[kk]],
            send_sem=p_sem.at[0, kk],
            recv_sem=p_sem.at[1, kk],
            device_id={"ch": across},
            device_id_type=MESH,
        )

    def combine(kk):
        hop(kk, 2, f_place, full, left).wait_recv()
        give[full[kk]] = partial(kk, 1).astype(BF16)
        push(share_out(kk))
        acc[full[kk]] = partial(kk, 0)

    for kk in range(last + 1):
        begin(kk)
    loads[5].wait()
    loads[6].wait()
    take(f_sem.at[1], lent)
    for kk in range(last + 1):
        relay(kk)
        combine(kk)
    stores = []
    for kk in range(last + 1):
        share_out(kk).wait_recv()
        span = full[kk]
        out_v[span] = (acc[span] + gain[span].astype(F32)).astype(BF16)
        stores.append(pltpu.make_async_copy(out_v.at[span], out.at[span], out_sem.at[kk]))
        stores[-1].start()

    edge.wait_send()
    take(h_sem.at[0], send_h.at[others])
    take(x_sem.at[0], send_x.at[others])
    for side in range(HALVES):
        take(y_sem.at[side, 0], recv_y.at[side, others])
    take(w_sem.at[0], lent)
    take(f_sem.at[0], lent)
    for copy in sent:
        copy.wait_send()
    for store in stores:
        store.wait()


def local(streams, short_taps, filters, skip_gain, out_weight, *, table):
    n_ctx, n_ch = lax.axis_size("ctx"), lax.axis_size("ch")
    seg, _, chans = streams.shape
    share = chans // n_ctx
    cols = out_weight.shape[1] // n_ch
    tiles = seg // LANES
    slabs = pltpu.VMEM((n_ctx, share, seg), BF16)
    wing = seg // HALVES
    parts = pltpu.VMEM((seg, cols), BF16)
    chunks = len(SPLITS)
    dma = pltpu.SemaphoreType.DMA
    return pl.pallas_call(
        functools.partial(operator_kernel, n_ctx, n_ch),
        out_shape=jax.ShapeDtypeStruct((seg, cols), BF16),
        in_specs=[pl.BlockSpec(memory_space=pl.ANY)] * 6,
        out_specs=pl.BlockSpec(memory_space=pl.ANY),
        scratch_shapes=[
            pltpu.VMEM((3, seg, chans), BF16),
            pltpu.VMEM(short_taps.shape, F32),
            pltpu.VMEM((seg, chans), BF16),
            pltpu.VMEM((1, chans), F32),
            pltpu.VMEM((seg, 2 * seg), BF16),
            pltpu.VMEM((RING, 2, chans, cols), BF16),
            pltpu.VMEM((3, seg + 8, chans), F32),
            pltpu.VMEM((3, EDGE, chans), BF16),
            slabs,
            slabs,
            slabs,
            slabs,
            pltpu.VMEM((HALVES, 2, n_ctx // 2, share, wing), BF16),
            pltpu.VMEM((HALVES, n_ctx, share, wing), BF16),
            pltpu.VMEM((3, tiles, n_ctx, share, LANES), F32),
            pltpu.VMEM((3, tiles, n_ctx + LEAD, share, LANES), F32),
            pltpu.VMEM((2, n_ctx // 2 * share, 2 * seg), BF16),
            pltpu.VMEM((seg, chans), F32),
            pltpu.VMEM((seg, chans), F32),
            pltpu.VMEM((RING, seg, chans), BF16),
            parts,
            parts,
            pltpu.VMEM((seg, cols), F32),
            pltpu.VMEM((seg, cols), BF16),
            dma((7,)),
            dma((2,)),
            dma((2,)),
            dma((2,)),
            dma((HALVES, 2)),
            dma((2,)),
            dma((2,)),
            dma((chunks, 4)),
            dma((chunks, 4)),
            dma((2, chunks)),
            dma((chunks,)),
        ],
        compiler_params=pltpu.CompilerParams(
            collective_id=0, has_side_effects=True, vmem_limit_bytes=67043328
        ),
        name="hyena_operator",
    )(
        jnp.transpose(streams, (1, 0, 2)),
        short_taps,
        filters,
        skip_gain[None],
        table,
        out_weight,
    )


def solution(mesh):
    seg = 16384 // mesh.shape["ctx"]
    return jax.shard_map(
        functools.partial(local, table=half_table(2 * seg)),
        mesh=mesh,
        in_specs=(
            P("ctx", None, "ch"),
            P(None, None, "ch"),
            P("ctx", "ch"),
            P("ch"),
            P("ch", None),
        ),
        out_specs=P("ctx", "ch"),
        check_vma=False,
    )
```

time: 63.6 us -> 59 us (0.928)
  Pallas kernels: 61.4 us -> 57 us
    pallas_call x1, Pallas kernels: 61.4 us -> 57 us  [local(): pl.pallas_call(functools.partial(operator_kernel, n_ctx, n_ch), out_shape...]
where the time goes in v4:
time: 59 us; the launch traced here: 58.9 us
  Pallas kernels  57 us (97%)
  local copies, waits for them, and re-layouts  1.87 us (3%)
    pallas_call x1, Pallas kernels, local(): pl.pallas_call(functools.partial(operator_kernel, n_ctx, n_ch), out_shape...  57 us
    unnamed x1, local copies, waits for them, and re-layouts  1.87 us

profile of v4, /device:TPU:1, one launch (start us, length us, event | category | flops | bytes accessed | tf_op | source)
XLA Modules:
  0.0 58.9 jit_solution(11102894666654291889)
XLA Ops:
  0.0 57.0 %hyena_operator.1 = bf16[512,512]{1,0:T(8,128)(2,1)} custom-call(bf16[3,512,256]{2,1,0:T(8,128)(2,1)} %bitcast.2, f32[3,3,256]{2,1,0:T(4,128)} %taps_in.1, bf16[512,256]{1,0:T(8,128)(2,1)} %filters.1, f32[1,256]{1,0:T(1,128)} %bitcast.3, bf16[512,1024]{1,0:T(8,128)(2,1)} %constant.2.clone.table_in, bf16[256,4096]{1,0:T(8,128)(2,1)} %weight.1), custom_call_target="tpu_custom_call" | custom-call | tf_op jit(solution)/shard_map/hyena_operator/pallas_call | solution.py:450
  57.0 1.9 %copy.8 = bf16[512,512]{1,0:T(8,128)(2,1)} copy(bf16[512,512]{1,0:T(8,128)(2,1)} %hyena_operator.1) | data formatting | bytes 1048576

commit v5 on v4

--- a/solution.py
+++ b/solution.py
@@ -257,10 +257,14 @@
             device_id_type=MESH,
         ).start()
 
+    def reach(k, count):
+        turn, spot = lax.div(k + 1, 4), lax.rem(k + 1, 4)
+        ahead = count // 4 + jnp.where(spot < 2, turn, -turn)
+        return jnp.where(lax.rem(spot, 2) == 0, ahead, count - ahead)
+
     def exchange(source, target, sem):
         def one(k, _):
-            reach = lax.div(k + 1, 2)
-            there = lax.rem(me + jnp.where(lax.rem(k, 2) == 1, reach, n_ctx - reach), n_ctx)
+            there = lax.rem(me + reach(k, n_ctx), n_ctx)
             slab(source.at[there], target, sem, there)
             return 0
 
@@ -311,8 +315,7 @@
             send_y[side, parity] = part.reshape(pairs, share, wing).astype(BF16)
 
             def back(k, _, side=side, parity=parity):
-                reach = lax.div(k + 1, 2)
-                pair = lax.rem(mine + jnp.where(lax.rem(k, 2) == 1, reach, pairs - reach), pairs)
+                pair = lax.rem(mine + jnp.where(k < pairs, reach(k, pairs), 0), pairs)
                 there = 2 * pair + parity
 
                 @pl.when(there != me)
@@ -323,7 +326,7 @@
 
                 return 0
 
-            lax.fori_loop(0, pairs, back, 0)
+            lax.fori_loop(1, pairs + 1, back, 0)
     for side in range(HALVES):
         recv_y[side, me] = send_y[side, core, mine]
 

time: 59 us -> 58.1 us (0.985)
  Pallas kernels: 57 us -> 56.1 us
    pallas_call x1, Pallas kernels: 57 us -> 56.1 us  [local(): pl.pallas_call(functools.partial(operator_kernel, n_ctx, n_ch), out_shape...]
where the time goes in v5:
time: 58.1 us; the launch traced here: 58 us
  Pallas kernels  56.1 us (97%)
  local copies, waits for them, and re-layouts  1.87 us (3%)
    pallas_call x1, Pallas kernels, local(): pl.pallas_call(functools.partial(operator_kernel, n_ctx, n_ch), out_shape...  56.1 us
    unnamed x1, local copies, waits for them, and re-layouts  1.87 us

profile of v5, /device:TPU:1, one launch (start us, length us, event | category | flops | bytes accessed | tf_op | source)
XLA Modules:
  0.0 58.0 jit_solution(4387929189723008457)
XLA Ops:
  0.0 56.1 %hyena_operator.1 = bf16[512,512]{1,0:T(8,128)(2,1)} custom-call(bf16[3,512,256]{2,1,0:T(8,128)(2,1)} %bitcast.2, f32[3,3,256]{2,1,0:T(4,128)} %taps_in.1, bf16[512,256]{1,0:T(8,128)(2,1)} %filters.1, f32[1,256]{1,0:T(1,128)} %bitcast.3, bf16[512,1024]{1,0:T(8,128)(2,1)} %constant.2.clone.table_in, bf16[256,4096]{1,0:T(8,128)(2,1)} %weight.1), custom_call_target="tpu_custom_call" | custom-call | tf_op jit(solution)/shard_map/hyena_operator/pallas_call | solution.py:453
  56.1 1.9 %copy.8 = bf16[512,512]{1,0:T(8,128)(2,1)} copy(bf16[512,512]{1,0:T(8,128)(2,1)} %hyena_operator.1) | data formatting | bytes 1048576

commit v6 on v5

--- a/solution.py
+++ b/solution.py
@@ -129,7 +129,8 @@
     skip_in,
     table_in,
     weight,
-    out,
+    own_out,
+    gain,
     strm,
     taps,
     filt,
@@ -151,9 +152,7 @@
     direct,
     gat,
     give,
-    gain,
     acc,
-    out_v,
     local_sem,
     halo_sem,
     h_sem,
@@ -198,10 +197,14 @@
 
     barrier = pltpu.get_barrier_semaphore()
 
+    def reach(k, count):
+        turn, spot = lax.div(k + 1, 4), lax.rem(k + 1, 4)
+        ahead = count // 4 + jnp.where(spot < 2, turn, -turn)
+        return jnp.where(lax.rem(spot, 2) == 0, ahead, count - ahead)
+
     def greet_ctx(k, _):
-        pl.semaphore_signal(
-            barrier, inc=1, device_id={"ctx": lax.rem(me + k, n_ctx)}, device_id_type=MESH
-        )
+        there = lax.rem(me + reach(k, n_ctx), n_ctx)
+        pl.semaphore_signal(barrier, inc=1, device_id={"ctx": there}, device_id_type=MESH)
         return 0
 
     def greet_ch(k, _):
@@ -256,11 +259,6 @@
             device_id={"ctx": there},
             device_id_type=MESH,
         ).start()
-
-    def reach(k, count):
-        turn, spot = lax.div(k + 1, 4), lax.rem(k + 1, 4)
-        ahead = count // 4 + jnp.where(spot < 2, turn, -turn)
-        return jnp.where(lax.rem(spot, 2) == 0, ahead, count - ahead)
 
     def exchange(source, target, sem):
         def one(k, _):
@@ -367,6 +365,7 @@
         )
 
     sent = []
+    stores = []
 
     def push(copy):
         copy.start()
@@ -384,15 +383,11 @@
         push(hop(kk, 1, place, full, left))
         push(hop(kk, 2, place, full, base + f_place))
 
-    def relay(kk):
-        hop(kk, 0, l_place, full, left).wait_recv()
-        hop(kk, 1, r_place, full, right).wait_recv()
-
-    def partial(kk, side):
-        total = jnp.dot(gat[place, full[kk]], wide[place, side], preferred_element_type=F32)
-        for block in (l_place, r_place, f_place):
-            total += jnp.dot(gat[block, full[kk]], wide[block, side], preferred_element_type=F32)
-        return total
+    def times(kk, block, side):
+        return jnp.dot(gat[block, full[kk]], wide[block, side], preferred_element_type=F32)
+
+    def near(kk, side):
+        return times(kk, place, side) + times(kk, l_place, side) + times(kk, r_place, side)
 
     def share_out(kk):
         return pltpu.make_async_remote_copy(
@@ -405,10 +400,16 @@
         )
 
     def combine(kk):
+        hop(kk, 0, l_place, full, left).wait_recv()
+        hop(kk, 1, r_place, full, right).wait_recv()
+        theirs = near(kk, 1)
         hop(kk, 2, f_place, full, left).wait_recv()
-        give[full[kk]] = partial(kk, 1).astype(BF16)
+        give[full[kk]] = (theirs + times(kk, f_place, 1)).astype(BF16)
         push(share_out(kk))
-        acc[full[kk]] = partial(kk, 0)
+        acc[full[kk]] = near(kk, 0) + times(kk, f_place, 0)
+        keep = pltpu.make_async_copy(acc.at[full[kk]], own_out.at[full[kk]], out_sem.at[kk])
+        keep.start()
+        stores.append(keep)
 
     for kk in range(last + 1):
         begin(kk)
@@ -416,15 +417,9 @@
     loads[6].wait()
     take(f_sem.at[1], lent)
     for kk in range(last + 1):
-        relay(kk)
         combine(kk)
-    stores = []
     for kk in range(last + 1):
         share_out(kk).wait_recv()
-        span = full[kk]
-        out_v[span] = (acc[span] + gain[span].astype(F32)).astype(BF16)
-        stores.append(pltpu.make_async_copy(out_v.at[span], out.at[span], out_sem.at[kk]))
-        stores[-1].start()
 
     edge.wait_send()
     take(h_sem.at[0], send_h.at[others])
@@ -450,11 +445,14 @@
     parts = pltpu.VMEM((seg, cols), BF16)
     chunks = len(SPLITS)
     dma = pltpu.SemaphoreType.DMA
-    return pl.pallas_call(
+    own, gained = pl.pallas_call(
         functools.partial(operator_kernel, n_ctx, n_ch),
-        out_shape=jax.ShapeDtypeStruct((seg, cols), BF16),
+        out_shape=[
+            jax.ShapeDtypeStruct((seg, cols), F32),
+            jax.ShapeDtypeStruct((seg, cols), BF16),
+        ],
         in_specs=[pl.BlockSpec(memory_space=pl.ANY)] * 6,
-        out_specs=pl.BlockSpec(memory_space=pl.ANY),
+        out_specs=[pl.BlockSpec(memory_space=pl.ANY)] * 2,
         scratch_shapes=[
             pltpu.VMEM((3, seg, chans), BF16),
             pltpu.VMEM(short_taps.shape, F32),
@@ -477,9 +475,7 @@
             pltpu.VMEM((seg, chans), F32),
             pltpu.VMEM((RING, seg, chans), BF16),
             parts,
-            parts,
             pltpu.VMEM((seg, cols), F32),
-            pltpu.VMEM((seg, cols), BF16),
             dma((7,)),
             dma((2,)),
             dma((2,)),
@@ -504,6 +500,7 @@
         table,
         out_weight,
     )
+    return (own + gained.astype(F32)).astype(BF16)
 
 
 def solution(mesh):

time: 58.1 us -> 57.9 us (level)
  other arithmetic: 0 us -> 2.31 us
  local copies, waits for them, and re-layouts: 1.87 us -> 0 us
  Pallas kernels: 56.1 us -> 55.4 us
    convert_element_type x0 -> x1, other arithmetic: none -> 2.31 us  [local(): return (own + gained.astype(F32)).astype(BF16)]
    unnamed x1 -> x0, local copies, waits for them, and re-layouts: 1.87 us -> none
    pallas_call x1, Pallas kernels: 56.1 us -> 55.4 us  [local(): pl.pallas_call(functools.partial(operator_kernel, n_ctx, n_ch), out_shape...]
where the time goes in v6:
time: 57.9 us; the launch traced here: 57.8 us
  Pallas kernels  55.4 us (96%)
  other arithmetic  2.31 us (4%)
    pallas_call x1, Pallas kernels, local(): pl.pallas_call(functools.partial(operator_kernel, n_ctx, n_ch), out_shape...  55.4 us
    convert_element_type x1, other arithmetic, local(): return (own + gained.astype(F32)).astype(BF16)  2.31 us

profile of v6, /device:TPU:1, one launch (start us, length us, event | category | flops | bytes accessed | tf_op | source)
XLA Modules:
  0.0 57.8 jit_solution(5163421754299716167)
XLA Ops:
  0.0 55.4 %hyena_operator.1 = (f32[512,512]{1,0:T(8,128)}, bf16[512,512]{1,0:T(8,128)(2,1)}) custom-call(bf16[3,512,256]{2,1,0:T(8,128)(2,1)} %bitcast.2, f32[3,3,256]{2,1,0:T(4,128)} %taps_in.1, bf16[512,256]{1,0:T(8,128)(2,1)} %filters.1, f32[1,256]{1,0:T(1,128)} %bitcast.3, bf16[512,1024]{1,0:T(8,128)(2,1)} %constant.2.clone.table_in, bf16[256,4096]{1,0:T(8,128)(2,1)} %weight.1), custom_call_target="tpu_custom_call" | custom-call | tf_op jit(solution)/shard_map/hyena_operator/pallas_call | solution.py:448
  55.4 2.3 %add_convert_fusion = bf16[512,512]{1,0:T(8,128)(2,1)} fusion(f32[512,512]{1,0:T(8,128)} %get-tuple-element.7, bf16[512,512]{1,0:T(8,128)(2,1)} %get-tuple-element.8), kind=kLoop, calls=%fused_computation | loop fusion | flops 786432 | bytes 2097152 | tf_op jit(solution)/shard_map/convert_element_type | solution.py:503
